TPU v7x, 512 devices: a whole 4x4x16 slice. The times are simulated.
512 devices in a mesh: occ: 16 (over z), vir: 32 (over y, x, core).
Axes of the slice: x: 4, y: 4, z: 16, core: 2. Of those that a mesh axis runs over, the one named last changes fastest.
Arguments:
- amplitudes: bfloat16 [2048, 24576], P('vir', 'occ'), may hold values from -6 to 6
- tiles: bfloat16 [16, 32, 48, 9216], P('occ', 'vir'), may hold values from -0.09375 to 0.09375
- tile_map: int32 [16, 32, 48], P('occ', 'vir'), may hold values from 0 to 128, as said below
Outputs:
- residual: bfloat16 [2048, 24576], P('occ', 'vir')
Inputs may be any that keep to these rules, and one draw needn't show every extreme that they name: `tile_map`: in each device's list of 48 slots the live entries name distinct tile pairs and come first; the value 16 * 8 marks an empty slot; some device has all 48 slots live.
All inputs are finite; a program needn't handle non-finite values.
Results may differ from a plain program's by a relative error of at most 0.022.
Values may be sent and summed in bfloat16 or wider, within the bound.
A program may use at most 64 MiB of HBM per device.

v0:
```python
import jax
import jax.numpy as jnp
from jax import lax
from jax.sharding import PartitionSpec as P

TILE = 96
CON_TILES = 16
RES_TILES = 8


def densify(tiles, tile_map):
    slot_ids = tile_map.reshape(-1)
    slot_count = slot_ids.shape[0]
    flat_tiles = tiles.reshape(slot_count, TILE * TILE)
    pair_ids = jnp.arange(CON_TILES * RES_TILES, dtype=jnp.int32)
    onehot = (slot_ids[:, None] == pair_ids[None, :]).astype(jnp.bfloat16)
    placed = jnp.einsum("sp,sq->pq", onehot, flat_tiles, preferred_element_type=jnp.float32)
    placed = placed.astype(jnp.bfloat16).reshape(CON_TILES, RES_TILES, TILE, TILE)
    return placed.transpose(0, 2, 1, 3).reshape(CON_TILES * TILE, RES_TILES * TILE)


def per_device(amplitudes, tiles, tile_map):
    integral_block = densify(tiles, tile_map)
    gathered = lax.all_gather(amplitudes, "vir", axis=0, tiled=True)
    partial_value = jnp.dot(gathered, integral_block, preferred_element_type=jnp.float32)
    summed = lax.psum_scatter(
        partial_value.astype(jnp.bfloat16), "occ", scatter_dimension=0, tiled=True
    )
    return summed


def solution(mesh):
    in_specs = (P("vir", "occ"), P("occ", "vir", None, None), P("occ", "vir", None))
    out_specs = P("occ", "vir")
    return jax.shard_map(
        per_device, mesh=mesh, in_specs=in_specs, out_specs=out_specs, check_vma=False
    )
```

profile of v0, /device:TPU:6, one launch (start us, length us, event | category | flops | bytes accessed | tf_op | source)
XLA Modules:
  0.0 176.5 jit_solution(14336208742318066604)
XLA Ops:
  6.5 0.0 copy-start
  6.5 0.0 all-gather.2.cloned.1.call-start
  6.5 0.7 all-gather.2.cloned.1.call-update
  7.3 0.0 reduce-scatter.4.cloned.1.call-start
  7.3 0.4 copy-done
  7.7 1.5 convolution_convert_fusion
  9.2 4.2 %reshape.11 = bf16[16,8,96,96]{3,2,1,0:T(8,128)(2,1)} reshape(bf16[128,9216]{1,0:T(8,128)(2,1)S(1)} %convolution_convert_fusion) | data formatting | bytes 4718592 | tf_op jit(solution)/shard_map/reshape | solution.py:18
  13.4 4.8 %copy.12 = bf16[16,8,96,96]{3,1,2,0:T(8,128)(2,1)} copy(bf16[16,8,96,96]{3,2,1,0:T(8,128)(2,1)} %reshape.11) | data formatting | bytes 4718592 | tf_op jit(solution)/shard_map/reshape | solution.py:18
  18.3 5.0 %reshape.12 = bf16[1536,768]{1,0:T(8,128)(2,1)S(1)} reshape(bf16[16,96,8,96]{3,2,1,0:T(8,128)(2,1)} %bitcast.14) | data formatting | bytes 4718592 | tf_op jit(solution)/shard_map/reshape | solution.py:19
  23.3 55.3 %all-gather.2.cloned.1.call-done = bf16[2048,1536]{1,0:T(8,128)(2,1)} async-done(((bf16[64,1536]{1,0:T(8,128)(2,1)}), bf16[2048,1536]{1,0:T(8,128)(2,1)}) %all-gather.2.cloned.1.call-update) | async-done | bytes 6291472 | tf_op jit(solution)/shard_map/all_gather | solution.py:24
  78.6 9.5 %fusion = bf16[2048,768]{0,1:T(8,128)(2,1)} fusion(bf16[1536,768]{1,0:T(8,128)(2,1)S(1)} %reshape.12, bf16[2048,1536]{1,0:T(8,128)(2,1)} %all-gather.2.cloned.1.call-done), kind=kOutput, calls=%fused_computation.3 | convolution fusion | flops 4833411072 | bytes 11796480 | tf_op jit(solution)/shard_map/dot_general | solution.py:25
  88.0 4.6 %copy.9 = bf16[2048,768]{1,0:T(8,128)(2,1)} copy(bf16[2048,768]{0,1:T(8,128)(2,1)} %fusion) | data formatting | bytes 6291456
  92.7 0.0 reduce-scatter.4.cloned.1.call-update
  92.7 77.0 %reduce-scatter.4.cloned.1.call-done = bf16[128,768]{1,0:T(8,128)(2,1)} async-done(((bf16[2048,768]{1,0:T(8,128)(2,1)}), bf16[128,768]{1,0:T(8,128)(2,1)}) %reduce-scatter.4.cloned.1.call-update) | async-done | bytes 196624 | tf_op jit(solution)/shard_map/reduce_scatter | solution.py:26
Async XLA Ops:
  6.5 1.2 copy-start
  6.5 72.0 %all-gather.2.cloned.1.call-start = ((), (), s32[]{:S(2)}) async-start(), calls=%async_computation.1 | async-start | bytes 6488064 | tf_op jit(solution)/shard_map/all_gather | solution.py:24
  7.3 162.4 %reduce-scatter.4.cloned.1.call-start = ((), (), s32[]{:S(2)}) async-start(), calls=%async_computation.2 | async-start | bytes 3342336 | tf_op jit(solution)/shard_map/reduce_scatter | solution.py:26
Sparse Core Ops, SparseCore 0:
  10.5 68.0 all-gather.1
  92.8 76.8 reduce-scatter.3
where the time goes:
time: 177 us
  waiting for transfers between devices  133 us (75%)
  local copies, waits for them, and re-layouts  19.1 us (11%)
  between operations  13.4 us (8%)
  matrix products  11 us (6%)
    reduce_scatter x1, waiting for transfers between devices, per_device(): lax.psum_scatter(partial_value.astype(jnp.bfloat16), 'occ', scatter_dimen...  77 us
    all_gather x1, waiting for transfers between devices, per_device(): gathered = lax.all_gather(amplitudes, 'vir', axis=0, tiled=True)  55.3 us
    dot_general x1, matrix products, per_device(): jnp.dot(gathered, integral_block, preferred_element_type=jnp.float32)  9.46 us
    reshape x2, local copies, waits for them, and re-layouts, densify(): placed.astype(jnp.bfloat16).reshape(CON_TILES, RES_TILES, TILE, TILE)  9.03 us
    unnamed x3, local copies, waits for them, and re-layouts  5.05 us
    reshape x1, local copies, waits for them, and re-layouts, densify(): placed.transpose(0, 2, 1, 3).reshape(CON_TILES * TILE, RES_TILES * TILE)  4.99 us
  transfers between devices with their start and end apart: 2, of which 2 were waited for; matrix products, arithmetic and copies ran while one was open for 9% of the time, Pallas kernels for 0%

commit v1 on v0

v1 whole, which is shorter than its diff:
```python
import jax
import jax.numpy as jnp
from jax import lax
from jax.experimental import pallas as pl
from jax.experimental.pallas import tpu as pltpu
from jax.sharding import PartitionSpec as P

TILE = 96
CON_TILES = 16
RES_TILES = 8
SLOTS = 48
NZ = 16
SIDE = 4
SHARD = 64
DEPTH = CON_TILES * TILE
WIDTH = RES_TILES * TILE
GROUP = 16
HALF = SHARD // 2
COLS = 256
MESH = pl.DeviceIdType.MESH
BF16, F32 = jnp.bfloat16, jnp.float32


def kernel(
    a_hbm, tiles_hbm, map_ref, out_ref,
    a_all, tiles_v, dense, acc, snd, rcv,
    local_sem, line_send, line_recv, plane_send, plane_recv, pair_send, pair_recv, ring_send, ring_recv,
):
    o = lax.axis_index("occ")
    v = lax.axis_index("vir")
    h = lax.rem(v, 2)
    chip = v // 2
    x, y = lax.rem(chip, SIDE), chip // SIDE
    first_x, first_y = 1 - h, h

    def vir_at(dx, dy):
        xx, yy = lax.rem(x + dx + SIDE, SIDE), lax.rem(y + dy + SIDE, SIDE)
        return (yy * SIDE + xx) * 2 + h

    def chip_at(step):
        xx, yy = lax.rem(x + step * first_x, SIDE), lax.rem(y + step * first_y, SIDE)
        return yy * SIDE + xx

    line_up, line_down = vir_at(first_x, first_y), vir_at(-first_x, -first_y)
    plane_up, plane_down = vir_at(first_y, first_x), vir_at(-first_y, -first_x)
    mate = chip * 2 + 1 - h
    ring = (lax.rem(o + 1, NZ), lax.rem(o + NZ - 1, NZ))

    def remote(src, dst, send, recv, device):
        return pltpu.make_async_remote_copy(
            src_ref=src, dst_ref=dst, send_sem=send, recv_sem=recv, device_id=device, device_id_type=MESH
        )

    tiles_copy = pltpu.make_async_copy(tiles_hbm, tiles_v, local_sem.at[0])
    own_copy = pltpu.make_async_copy(a_hbm, a_all.at[chip, h], local_sem.at[1])
    tiles_copy.start()
    own_copy.start()

    barrier = pltpu.get_barrier_semaphore()
    for device in (line_up, line_down, plane_up, plane_down, mate):
        pl.semaphore_signal(barrier, inc=1, device_id={"vir": device}, device_id_type=MESH)
    for device in ring:
        pl.semaphore_signal(barrier, inc=1, device_id={"occ": device}, device_id_type=MESH)
    pl.semaphore_wait(barrier, 7)

    def line_full(k):
        device = line_up if k == 0 else line_down
        return remote(a_hbm, a_all.at[chip, h], line_send.at[k], line_recv.at[k], {"vir": device})

    def line_got(k):
        c = chip_at(3 if k == 0 else 1)
        return c, remote(a_hbm, a_all.at[c, h], line_send.at[k], line_recv.at[k], {"vir": line_up})

    def line_half(k):
        c = chip_at(3 if k == 0 else 1)
        part = a_all.at[c, h, pl.ds(k * HALF, HALF)]
        device = line_up if k == 0 else line_down
        return remote(part, part, line_send.at[2 + k], line_recv.at[2 + k], {"vir": device})

    def line_last(k):
        part = a_all.at[chip_at(2), h, pl.ds(k * HALF, HALF)]
        return remote(part, part, line_send.at[2 + k], line_recv.at[2 + k], {"vir": line_up})

    def where(c):
        xc, yc = lax.rem(c, SIDE), c // SIDE
        mine = y + h * (x - y)
        owner = yc + h * (xc - yc)
        return lax.rem(mine - owner + SIDE, SIDE)

    def plane_full(c, k):
        device = plane_up if k == 0 else plane_down
        part = a_all.at[c, h]
        return remote(part, part, plane_send.at[k, c], plane_recv.at[0, c], {"vir": device})

    def plane_half(c, k):
        device = plane_up if k == 0 else plane_down
        part = a_all.at[c, h, pl.ds(k * HALF, HALF)]
        return remote(part, part, plane_send.at[k, c], plane_recv.at[k, c], {"vir": device})

    def pair(c):
        part = a_all.at[c, h]
        return remote(part, part, pair_send.at[c], pair_recv.at[c], {"vir": mate})

    def pair_got(c):
        part = a_all.at[c, 1 - h]
        return remote(part, part, pair_send.at[c], pair_recv.at[c], {"vir": mate})

    def chunk(r):
        odd = lax.rem(r, 2)
        d = 8 + (1 - 2 * odd) * ((r + 1) // 2)
        return lax.rem(o + d, NZ)

    def plane_out(r):
        c = chunk(r)

        @pl.when(where(c) == 0)
        def _():
            plane_full(c, 0).start()
            plane_full(c, 1).start()
            pair(c).start()

    def plane_in(r):
        c = chunk(r)
        at = where(c)

        @pl.when(at == 1)
        def _():
            plane_full(c, 0).wait_recv()
            plane_half(c, 0).start()
            pair(c).start()

        @pl.when(at == 3)
        def _():
            plane_full(c, 0).wait_recv()
            plane_half(c, 1).start()
            pair(c).start()

        @pl.when(at == 2)
        def _():
            plane_half(c, 0).wait_recv()
            plane_half(c, 1).wait_recv()
            pair(c).start()

    pairs = lax.broadcasted_iota(jnp.int32, (CON_TILES * RES_TILES, SLOTS), 0)
    pairs = (pairs & 15) * RES_TILES + (pairs >> 4)
    select = jnp.where(map_ref[...] == pairs, 1.0, 0.0).astype(BF16)
    row = lax.broadcasted_iota(jnp.int32, (256, 256), 0)
    col = lax.broadcasted_iota(jnp.int32, (256, 256), 1)
    swap = jnp.where(col == (row & 15) * 16 + (row >> 4), 1.0, 0.0).astype(BF16)

    def densify(kb):
        start = pl.multiple_of(kb * GROUP * TILE, GROUP * TILE)
        flat = tiles_v[:, pl.ds(start, GROUP * TILE)]
        placed = jnp.dot(select, flat, preferred_element_type=F32).astype(BF16)
        rows = [
            jnp.concatenate(
                [placed[t * 16:(t + 1) * 16, k * TILE:(k + 1) * TILE] for t in range(RES_TILES)], axis=1
            )
            for k in range(GROUP)
        ]
        mixed = jnp.concatenate(rows, axis=0)
        done = jnp.dot(swap, mixed, preferred_element_type=F32).astype(BF16)
        for c in range(CON_TILES):
            at = pl.multiple_of(c * TILE + kb * GROUP, GROUP)
            dense[pl.ds(at, GROUP), :] = done[c * GROUP:(c + 1) * GROUP, :]

    def densify_range(low, high):
        def body(kb, carry):
            densify(kb)
            return carry

        lax.fori_loop(low, high, body, 0)

    def multiply(c, arm):
        for n in range(0, WIDTH, COLS):
            acc[arm, :, n:n + COLS] = jnp.dot(
                a_all[c].reshape(2 * SHARD, DEPTH), dense[:, n:n + COLS], preferred_element_type=F32
            )

    def hop(arm, s, sub):
        return remote(
            snd.at[arm, s, sub], rcv.at[arm, s, sub], ring_send.at[arm, s, sub], ring_recv.at[arm, s, sub],
            {"occ": ring[arm]},
        )

    def pass_on(arm, s, sub, add):
        value = acc[arm, sub * SHARD:(sub + 1) * SHARD, :]
        if add:
            hop(arm, s - 1, sub).wait_recv()
            value = value + rcv[arm, s - 1, sub].astype(F32)
        snd[arm, s, sub] = value.astype(BF16)
        hop(arm, s, sub).start()

    def ring_step(s, first):
        for arm in (0, 1):
            d = (8 - s) if arm == 0 else (8 + s)
            c = lax.rem(o + d, NZ)
            pair_got(c).wait_recv()
            multiply(c, arm)
        pass_on(0, s, 0, True)
        pass_on(1, s, 1, True)
        pass_on(0, s, 1, not first)
        pass_on(1, s, 0, not first)

    line_full(0).start()
    line_full(1).start()
    tiles_copy.wait()
    densify_range(0, 3)
    for k in (0, 1):
        line_got(k)[1].wait_recv()
        line_half(k).start()
    own_copy.wait()
    densify_range(3, 5)
    for k in (0, 1):
        line_last(k).wait_recv()
    for r in range(4):
        plane_out(r)
    densify_range(5, 6)
    plane_out(4)
    plane_in(0)
    c0 = chunk(0)
    pair_got(c0).wait_recv()
    multiply(c0, 0)
    for arm in (0, 1):
        snd[arm, 0, arm] = acc[0, arm * SHARD:(arm + 1) * SHARD, :].astype(BF16)
        hop(arm, 0, arm).start()

    def plane_body(r, carry):
        @pl.when(r + 4 < NZ)
        def _():
            plane_out(r + 4)

        plane_in(r)
        return carry

    lax.fori_loop(1, 5, plane_body, 0)
    ring_step(1, True)
    lax.fori_loop(5, 7, plane_body, 0)

    def body(s, carry):
        ring_step(s, False)
        lax.fori_loop(jnp.minimum(2 * s + 3, NZ), jnp.minimum(2 * s + 5, NZ), plane_body, 0)
        return carry

    lax.fori_loop(2, 8, body, 0)

    pair_got(o).wait_recv()
    multiply(o, 0)
    for sub in (0, 1):
        hop(0, 7, sub).wait_recv()
        hop(1, 7, sub).wait_recv()
        value = acc[0, sub * SHARD:(sub + 1) * SHARD, :]
        value = value + rcv[0, 7, sub].astype(F32) + rcv[1, 7, sub].astype(F32)
        out_ref[sub * SHARD:(sub + 1) * SHARD, :] = value.astype(BF16)

    for k in (0, 1):
        line_full(k).wait_send()
        line_half(k).wait_send()

    def drain(c, carry):
        at = where(c)
        pair(c).wait_send()

        @pl.when(at == 0)
        def _():
            plane_full(c, 0).wait_send()
            plane_full(c, 1).wait_send()

        @pl.when(at == 1)
        def _():
            plane_half(c, 0).wait_send()

        @pl.when(at == 3)
        def _():
            plane_half(c, 1).wait_send()

        return carry

    lax.fori_loop(0, NZ, drain, 0)
    for arm in (0, 1):
        hop(arm, 0, arm).wait_send()

    def drain_ring(s, carry):
        for arm in (0, 1):
            for sub in (0, 1):
                hop(arm, s, sub).wait_send()
        return carry

    lax.fori_loop(1, 8, drain_ring, 0)


def per_device(amplitudes, tiles, tile_map):
    dma = pltpu.SemaphoreType.DMA
    return pl.pallas_call(
        kernel,
        out_shape=jax.ShapeDtypeStruct((2 * SHARD, WIDTH), BF16),
        in_specs=[
            pl.BlockSpec(memory_space=pl.ANY),
            pl.BlockSpec(memory_space=pl.ANY),
            pl.BlockSpec(memory_space=pltpu.VMEM),
        ],
        out_specs=pl.BlockSpec(memory_space=pltpu.VMEM),
        scratch_shapes=[
            pltpu.VMEM((NZ, 2, SHARD, DEPTH), BF16),
            pltpu.VMEM((SLOTS, TILE * TILE), BF16),
            pltpu.VMEM((DEPTH, WIDTH), BF16),
            pltpu.VMEM((2, 2 * SHARD, WIDTH), F32),
            pltpu.VMEM((2, 8, 2, SHARD, WIDTH), BF16),
            pltpu.VMEM((2, 8, 2, SHARD, WIDTH), BF16),
            dma((2,)),
            dma((4,)),
            dma((4,)),
            dma((2, NZ)),
            dma((2, NZ)),
            dma((NZ,)),
            dma((NZ,)),
            dma((2, 8, 2)),
            dma((2, 8, 2)),
        ],
        compiler_params=pltpu.CompilerParams(
            collective_id=0, has_side_effects=True, vmem_limit_bytes=48 * 1024 * 1024
        ),
    )(amplitudes, tiles.reshape(SLOTS, TILE * TILE), tile_map.reshape(1, SLOTS))


def solution(mesh):
    in_specs = (P("vir", "occ"), P("occ", "vir", None, None), P("occ", "vir", None))
    out_specs = P("occ", "vir")
    return jax.shard_map(
        per_device, mesh=mesh, in_specs=in_specs, out_specs=out_specs, check_vma=False
    )
```

time: 177 us -> 115 us (0.65)
  the two profiles are of different devices: /device:TPU:6 before, /device:TPU:10 now
where the time goes in v1:
time: 115 us
  Pallas kernels  112 us (97%)
  local copies, waits for them, and re-layouts  3.43 us (3%)
    pallas_call x1, Pallas kernels, per_device(): pl.pallas_call(kernel, out_shape=jax.ShapeDtypeStruct((2 * SHARD, WIDTH),...  112 us
    unnamed x7, local copies, waits for them, and re-layouts  3.43 us

profile of v1, /device:TPU:10, one launch (start us, length us, event | category | flops | bytes accessed | tf_op | source)
XLA Modules:
  0.0 115.0 jit_solution(7795707317875102865)
XLA Ops:
  0.0 0.0 copy-start.2
  0.0 0.7 copy-done.2
  0.7 0.0 copy-start
  0.7 1.2 %copy-done = bf16[1,1,48,9216]{3,2,1,0:T(8,128)(2,1)S(1)} copy-done((bf16[1,1,48,9216]{3,2,1,0:T(8,128)(2,1)S(1)}, bf16[1,1,48,9216]{3,2,1,0:T(8,128)(2,1)}, u32[]{:S(2)}) %copy-start) | copy-done | bytes 884760
  1.8 0.0 copy-start.1
  1.8 0.9 copy-done.1
  2.8 111.6 %shard_map.37 = bf16[128,768]{1,0:T(8,128)(2,1)S(1)} custom-call(bf16[64,1536]{1,0:T(8,128)(2,1)S(1)} %copy-done.1, bf16[48,9216]{1,0:T(8,128)(2,1)S(1)} %bitcast.2, s32[1,48]{1,0:T(1,128)S(1)} %bitcast.3), custom_call_target="tpu_custom_call" | custom-call | tf_op jit(solution)/shard_map/pallas_call | solution.py:294
  114.3 0.7 copy.5
Async XLA Ops:
  0.0 0.7 copy-start.2
  0.7 1.2 %copy-start = (bf16[1,1,48,9216]{3,2,1,0:T(8,128)(2,1)S(1)}, bf16[1,1,48,9216]{3,2,1,0:T(8,128)(2,1)}, u32[]{:S(2)}) copy-start(bf16[1,1,48,9216]{3,2,1,0:T(8,128)(2,1)} %param.4) | copy-start | bytes 2654212
  1.8 0.9 copy-start.1

commit v2 on v1

v2 whole, which is shorter than its diff:
```python
import jax
import jax.numpy as jnp
from jax import lax
from jax.experimental import pallas as pl
from jax.experimental.pallas import tpu as pltpu
from jax.sharding import PartitionSpec as P

TILE = 96
CON_TILES = 16
RES_TILES = 8
SLOTS = 48
NZ = 16
SIDE = 4
SHARD = 64
DEPTH = CON_TILES * TILE
WIDTH = RES_TILES * TILE
GROUP = 16
PIECES = 2
PIECE = SHARD // PIECES
SUBS = 4
SUB = 2 * SHARD // SUBS
AHEAD = 6
EARLY = 3
OTHERS = (1, 3, 2)
COLS = 256
MESH = pl.DeviceIdType.MESH
BF16, F32 = jnp.bfloat16, jnp.float32


def kernel(
    a_hbm, tiles_hbm, map_ref, out_ref,
    a_all, tiles_v, dense, acc, snd, rcv,
    local_sem, line_send, line_recv, plane_send, plane_recv, pair_send, pair_recv, ring_send, ring_recv,
):
    o = lax.axis_index("occ")
    v = lax.axis_index("vir")
    h = lax.rem(v, 2)
    chip = v // 2
    x, y = lax.rem(chip, SIDE), chip // SIDE
    first_x, first_y = 1 - h, h

    def vir_at(dx, dy):
        xx, yy = lax.rem(x + dx, SIDE), lax.rem(y + dy, SIDE)
        return (yy * SIDE + xx) * 2 + h

    def chip_at(step):
        xx, yy = lax.rem(x + step * first_x, SIDE), lax.rem(y + step * first_y, SIDE)
        return yy * SIDE + xx

    def on_line(k):
        return {"vir": vir_at(k * first_x, k * first_y)}

    def on_plane(k):
        return {"vir": vir_at(k * first_y, k * first_x)}

    mate = {"vir": chip * 2 + 1 - h}
    ring = ({"occ": lax.rem(o + 1, NZ)}, {"occ": lax.rem(o + NZ - 1, NZ)})

    def remote(src, dst, send, recv, device):
        return pltpu.make_async_remote_copy(
            src_ref=src, dst_ref=dst, send_sem=send, recv_sem=recv, device_id=device, device_id_type=MESH
        )

    tiles_copy = pltpu.make_async_copy(tiles_hbm, tiles_v, local_sem.at[0])
    own_copy = pltpu.make_async_copy(a_hbm, a_all.at[chip, h], local_sem.at[1])
    tiles_copy.start()
    own_copy.start()

    barrier = pltpu.get_barrier_semaphore()
    for device in [on_line(k) for k in OTHERS] + [on_plane(k) for k in OTHERS] + [mate, *ring]:
        pl.semaphore_signal(barrier, inc=1, device_id=device, device_id_type=MESH)
    pl.semaphore_wait(barrier, 9)

    def rows(p):
        return pl.ds(p * PIECE, PIECE)

    def line(k, p):
        return remote(
            a_hbm.at[rows(p)], a_all.at[chip, h, rows(p)], line_send.at[k, p], line_recv.at[k, p], on_line(k)
        )

    def line_got(c, k, p):
        part = a_all.at[c, h, rows(p)]
        return remote(part, part, line_send.at[k, p], line_recv.at[k, p], on_line(k))

    def plane(c, k, p):
        part = a_all.at[c, h, rows(p)]
        return remote(part, part, plane_send.at[c, k, p], plane_recv.at[c, p], on_plane(k))

    def pair(c):
        part = a_all.at[c, h]
        return remote(part, part, pair_send.at[c], pair_recv.at[c], mate)

    def pair_got(c):
        part = a_all.at[c, 1 - h]
        return remote(part, part, pair_send.at[c], pair_recv.at[c], mate)

    def steps_from(c):
        xc, yc = lax.rem(c, SIDE), c // SIDE
        line_steps = first_x * (x - xc) + first_y * (y - yc)
        plane_steps = first_y * (x - xc) + first_x * (y - yc)
        return lax.rem(line_steps + SIDE, SIDE), lax.rem(plane_steps + SIDE, SIDE)

    def chunk(r):
        odd = lax.rem(r, 2)
        d = 8 + (1 - 2 * odd) * ((r + 1) // 2)
        return lax.rem(o + d, NZ)

    def plane_out(r):
        c = chunk(r)
        near, far = steps_from(c)

        @pl.when(far == 0)
        def _():
            for p in range(PIECES):
                @pl.when(near != 0)
                def _():
                    line_got(c, near, p).wait_recv()

                for k in OTHERS:
                    plane(c, k, p).start()

    def fetch(r):
        c = chunk(r)

        @pl.when(steps_from(c)[1] != 0)
        def _():
            for p in range(PIECES):
                plane(c, 1, p).wait_recv()

        pair(c).start()

    pairs = lax.broadcasted_iota(jnp.int32, (CON_TILES * RES_TILES, SLOTS), 0)
    pairs = (pairs & 15) * RES_TILES + (pairs >> 4)
    select = jnp.where(map_ref[...] == pairs, 1.0, 0.0).astype(BF16)
    row = lax.broadcasted_iota(jnp.int32, (256, 256), 0)
    col = lax.broadcasted_iota(jnp.int32, (256, 256), 1)
    swap = jnp.where(col == (row & 15) * 16 + (row >> 4), 1.0, 0.0).astype(BF16)

    def densify(kb):
        start = pl.multiple_of(kb * GROUP * TILE, GROUP * TILE)
        flat = tiles_v[:, pl.ds(start, GROUP * TILE)]
        placed = jnp.dot(select, flat, preferred_element_type=F32).astype(BF16)
        rows = [
            jnp.concatenate(
                [placed[t * 16:(t + 1) * 16, k * TILE:(k + 1) * TILE] for t in range(RES_TILES)], axis=1
            )
            for k in range(GROUP)
        ]
        mixed = jnp.concatenate(rows, axis=0)
        done = jnp.dot(swap, mixed, preferred_element_type=F32).astype(BF16)
        for c in range(CON_TILES):
            at = pl.multiple_of(c * TILE + kb * GROUP, GROUP)
            dense[pl.ds(at, GROUP), :] = done[c * GROUP:(c + 1) * GROUP, :]

    def densify_range(low, high):
        def body(kb, carry):
            densify(kb)
            return carry

        lax.fori_loop(low, high, body, 0)

    def multiply(c, arm):
        for n in range(0, WIDTH, COLS):
            acc[arm, :, n:n + COLS] = jnp.dot(
                a_all[c].reshape(2 * SHARD, DEPTH), dense[:, n:n + COLS], preferred_element_type=F32
            )

    def hop(arm, s, sub):
        return remote(
            snd.at[arm, s, sub], rcv.at[arm, s, sub], ring_send.at[arm, s, sub], ring_recv.at[arm, s, sub],
            ring[arm],
        )

    def own(arm, sub):
        return acc[arm, sub * SUB:(sub + 1) * SUB, :]

    def pass_on(arm, s, sub, add):
        value = own(arm, sub)
        if add:
            hop(arm, s - 1, sub).wait_recv()
            value = value + rcv[arm, s - 1, sub].astype(F32)
        snd[arm, s, sub] = value.astype(BF16)
        hop(arm, s, sub).start()

    half = SUBS // 2
    long = (tuple(range(half)), tuple(range(half, SUBS)))
    short = (long[1], long[0])

    def ring_step(s, first):
        for arm in (0, 1):
            d = (8 - s) if arm == 0 else (8 + s)
            c = lax.rem(o + d, NZ)
            pair_got(c).wait_recv()
            multiply(c, arm)
        for i in range(half):
            for arm in (0, 1):
                pass_on(arm, s, long[arm][i], True)
        for i in range(half):
            for arm in (0, 1):
                pass_on(arm, s, short[arm][i], not first)

    def each(low, high, f):
        def body(i, carry):
            f(i)
            return carry

        lax.fori_loop(low, high, body, 0)

    def ahead(s):
        each(jnp.minimum(2 * s + AHEAD, NZ), jnp.minimum(2 * s + AHEAD + 2, NZ), plane_out)
        each(2 * s + 1, jnp.minimum(2 * s + 3, NZ), fetch)

    for p in range(PIECES):
        for k in OTHERS:
            line(k, p).start()
    tiles_copy.wait()
    densify_range(0, EARLY)
    own_copy.wait()
    each(0, AHEAD, plane_out)
    densify_range(EARLY, 6)
    fetch(0)
    c0 = chunk(0)
    pair_got(c0).wait_recv()
    multiply(c0, 0)
    for i in range(half):
        for arm in (0, 1):
            sub = long[arm][i]
            snd[arm, 0, sub] = own(0, sub).astype(BF16)
            hop(arm, 0, sub).start()
    ahead(0)
    ring_step(1, True)
    ahead(1)

    def body(s, carry):
        ring_step(s, False)
        ahead(s)
        return carry

    lax.fori_loop(2, 8, body, 0)

    pair_got(o).wait_recv()
    multiply(o, 0)
    for i in range(SUBS):
        sub = (long[0] + long[1])[i]
        hop(0, 7, sub).wait_recv()
        hop(1, 7, sub).wait_recv()
        value = own(0, sub) + rcv[0, 7, sub].astype(F32) + rcv[1, 7, sub].astype(F32)
        out_ref[sub * SUB:(sub + 1) * SUB, :] = value.astype(BF16)

    for p in range(PIECES):
        for k in OTHERS:
            line(k, p).wait_send()

    def drain(c):
        pair(c).wait_send()

        @pl.when(steps_from(c)[1] == 0)
        def _():
            for p in range(PIECES):
                for k in OTHERS:
                    plane(c, k, p).wait_send()

    each(0, NZ, drain)
    for arm in (0, 1):
        for sub in long[arm]:
            hop(arm, 0, sub).wait_send()

    def drain_ring(s):
        for arm in (0, 1):
            for sub in range(SUBS):
                hop(arm, s, sub).wait_send()

    each(1, 8, drain_ring)


def per_device(amplitudes, tiles, tile_map):
    dma = pltpu.SemaphoreType.DMA
    return pl.pallas_call(
        kernel,
        out_shape=jax.ShapeDtypeStruct((2 * SHARD, WIDTH), BF16),
        in_specs=[
            pl.BlockSpec(memory_space=pltpu.HBM),
            pl.BlockSpec(memory_space=pltpu.HBM),
            pl.BlockSpec(memory_space=pltpu.VMEM),
        ],
        out_specs=pl.BlockSpec(memory_space=pltpu.VMEM),
        scratch_shapes=[
            pltpu.VMEM((NZ, 2, SHARD, DEPTH), BF16),
            pltpu.VMEM((SLOTS, TILE * TILE), BF16),
            pltpu.VMEM((DEPTH, WIDTH), BF16),
            pltpu.VMEM((2, 2 * SHARD, WIDTH), F32),
            pltpu.VMEM((2, 8, SUBS, SUB, WIDTH), BF16),
            pltpu.VMEM((2, 8, SUBS, SUB, WIDTH), BF16),
            dma((2,)),
            dma((SIDE, PIECES)),
            dma((SIDE, PIECES)),
            dma((NZ, SIDE, PIECES)),
            dma((NZ, PIECES)),
            dma((NZ,)),
            dma((NZ,)),
            dma((2, 8, SUBS)),
            dma((2, 8, SUBS)),
        ],
        compiler_params=pltpu.CompilerParams(
            collective_id=0, has_side_effects=True, vmem_limit_bytes=61400 * 1024
        ),
    )(amplitudes, tiles.reshape(SLOTS, TILE * TILE), tile_map.reshape(1, SLOTS))


def solution(mesh):
    in_specs = (P("vir", "occ"), P("occ", "vir", None, None), P("occ", "vir", None))
    out_specs = P("occ", "vir")
    return jax.shard_map(
        per_device, mesh=mesh, in_specs=in_specs, out_specs=out_specs, check_vma=False
    )
```

time: 115 us -> 79.6 us (0.69)
  the two profiles are of different devices: /device:TPU:10 before, /device:TPU:1 now
where the time goes in v2:
time: 79.6 us; the launch traced here: 79.3 us
  Pallas kernels  77.7 us (98%)
  local copies, waits for them, and re-layouts  1.62 us (2%)
    pallas_call x1, Pallas kernels, per_device(): pl.pallas_call(kernel, out_shape=jax.ShapeDtypeStruct((2 * SHARD, WIDTH),...  77.7 us
    unnamed x1, local copies, waits for them, and re-layouts  1.62 us

profile of v2, /device:TPU:1, one launch (start us, length us, event | category | flops | bytes accessed | tf_op | source)
XLA Modules:
  0.0 79.3 jit_solution(8143483390810669467)
XLA Ops:
  0.0 77.7 %shard_map.37 = bf16[128,768]{1,0:T(8,128)(2,1)} custom-call(bf16[64,1536]{1,0:T(8,128)(2,1)} %a_hbm.1, bf16[48,9216]{1,0:T(8,128)(2,1)} %bitcast.2, s32[1,48]{1,0:T(1,128)} %bitcast.3), custom_call_target="tpu_custom_call" | custom-call | tf_op jit(solution)/shard_map/pallas_call | solution.py:279
  77.7 1.6 %copy.5 = bf16[128,768]{1,0:T(8,128)(2,1)} copy(bf16[128,768]{1,0:T(8,128)(2,1)} %shard_map.37) | data formatting | bytes 393216

commit v3 on v2

--- a/solution.py
+++ b/solution.py
@@ -19,17 +19,15 @@
 PIECE = SHARD // PIECES
 SUBS = 4
 SUB = 2 * SHARD // SUBS
-AHEAD = 6
-EARLY = 3
-OTHERS = (1, 3, 2)
+OTHERS = (2, 1, 3)
 COLS = 256
 MESH = pl.DeviceIdType.MESH
 BF16, F32 = jnp.bfloat16, jnp.float32
 
 
 def kernel(
-    a_hbm, tiles_hbm, map_ref, out_ref,
-    a_all, tiles_v, dense, acc, snd, rcv,
+    a_hbm, tiles_hbm, map_hbm, out_hbm,
+    a_all, tiles_v, map_ref, result, dense, acc, snd, rcv,
     local_sem, line_send, line_recv, plane_send, plane_recv, pair_send, pair_recv, ring_send, ring_recv,
 ):
     o = lax.axis_index("occ")
@@ -63,6 +61,8 @@
 
     tiles_copy = pltpu.make_async_copy(tiles_hbm, tiles_v, local_sem.at[0])
     own_copy = pltpu.make_async_copy(a_hbm, a_all.at[chip, h], local_sem.at[1])
+    map_copy = pltpu.make_async_copy(map_hbm, map_ref, local_sem.at[2])
+    map_copy.start()
     tiles_copy.start()
     own_copy.start()
 
@@ -106,20 +106,6 @@
         d = 8 + (1 - 2 * odd) * ((r + 1) // 2)
         return lax.rem(o + d, NZ)
 
-    def plane_out(r):
-        c = chunk(r)
-        near, far = steps_from(c)
-
-        @pl.when(far == 0)
-        def _():
-            for p in range(PIECES):
-                @pl.when(near != 0)
-                def _():
-                    line_got(c, near, p).wait_recv()
-
-                for k in OTHERS:
-                    plane(c, k, p).start()
-
     def fetch(r):
         c = chunk(r)
 
@@ -130,8 +116,101 @@
 
         pair(c).start()
 
+    def multiply(c, arm):
+        for n in range(0, WIDTH, COLS):
+            acc[arm, :, n:n + COLS] = jnp.dot(
+                a_all[c].reshape(2 * SHARD, DEPTH), dense[:, n:n + COLS], preferred_element_type=F32
+            )
+
+    def hop(arm, s, sub):
+        return remote(
+            snd.at[arm, s, sub], rcv.at[arm, s, sub], ring_send.at[arm, s, sub], ring_recv.at[arm, s, sub],
+            ring[arm],
+        )
+
+    def own(arm, sub):
+        return acc[arm, sub * SUB:(sub + 1) * SUB, :]
+
+    def pass_on(arm, s, sub, add):
+        value = own(arm, sub)
+        if add:
+            hop(arm, s - 1, sub).wait_recv()
+            value = value + rcv[arm, s - 1, sub].astype(F32)
+        snd[arm, s, sub] = value.astype(BF16)
+        hop(arm, s, sub).start()
+
+    half = SUBS // 2
+    long = (tuple(range(half)), tuple(range(half, SUBS)))
+    short = (long[1], long[0])
+
+    def ring_step(s, first):
+        for arm in (0, 1):
+            d = (8 - s) if arm == 0 else (8 + s)
+            c = lax.rem(o + d, NZ)
+            pair_got(c).wait_recv()
+            multiply(c, arm)
+        for i in range(half):
+            for arm in (0, 1):
+                pass_on(arm, s, long[arm][i], True)
+        for i in range(half):
+            for arm in (0, 1):
+                pass_on(arm, s, short[arm][i], not first)
+
+    def each(low, high, f):
+        def body(i, carry):
+            f(i)
+            return carry
+
+        lax.fori_loop(low, high, body, 0)
+
+    def rank(c):
+        away = lax.rem(c - o + NZ, NZ)
+        return jnp.where(away < 8, 15 - 2 * away, 2 * away - 16)
+
+    line_chips = [chip_at(k) for k in range(SIDE)]
+    line_ranks = [rank(c) for c in line_chips]
+    places = [
+        sum((line_ranks[j] < line_ranks[k]).astype(jnp.int32) for j in range(SIDE) if j != k) for k in range(SIDE)
+    ]
+
+    def line_out(place):
+        @pl.when(places[0] == place)
+        def _():
+            for p in range(PIECES):
+                for k in OTHERS:
+                    line(k, p).start()
+
+    def batch_out(place):
+        for k in range(SIDE):
+            @pl.when(places[k] == place)
+            def _():
+                for p in range(PIECES):
+                    if k != 0:
+                        line_got(line_chips[k], SIDE - k, p).wait_recv()
+                    for j in OTHERS:
+                        plane(line_chips[k], j, p).start()
+
+    def batch_sent(place):
+        for k in range(SIDE):
+            @pl.when(places[k] == place)
+            def _():
+                for p in range(PIECES):
+                    for j in OTHERS:
+                        plane(line_chips[k], j, p).wait_send()
+
+    def next_batch(i):
+        batch_sent(i - 1)
+        batch_out(i)
+
+    def ahead(s):
+        each(2 * s + 1, jnp.minimum(2 * s + 3, NZ), fetch)
+
+    for place in range(SIDE):
+        line_out(place)
+
     pairs = lax.broadcasted_iota(jnp.int32, (CON_TILES * RES_TILES, SLOTS), 0)
     pairs = (pairs & 15) * RES_TILES + (pairs >> 4)
+    map_copy.wait()
     select = jnp.where(map_ref[...] == pairs, 1.0, 0.0).astype(BF16)
     row = lax.broadcasted_iota(jnp.int32, (256, 256), 0)
     col = lax.broadcasted_iota(jnp.int32, (256, 256), 1)
@@ -160,65 +239,12 @@
 
         lax.fori_loop(low, high, body, 0)
 
-    def multiply(c, arm):
-        for n in range(0, WIDTH, COLS):
-            acc[arm, :, n:n + COLS] = jnp.dot(
-                a_all[c].reshape(2 * SHARD, DEPTH), dense[:, n:n + COLS], preferred_element_type=F32
-            )
-
-    def hop(arm, s, sub):
-        return remote(
-            snd.at[arm, s, sub], rcv.at[arm, s, sub], ring_send.at[arm, s, sub], ring_recv.at[arm, s, sub],
-            ring[arm],
-        )
-
-    def own(arm, sub):
-        return acc[arm, sub * SUB:(sub + 1) * SUB, :]
-
-    def pass_on(arm, s, sub, add):
-        value = own(arm, sub)
-        if add:
-            hop(arm, s - 1, sub).wait_recv()
-            value = value + rcv[arm, s - 1, sub].astype(F32)
-        snd[arm, s, sub] = value.astype(BF16)
-        hop(arm, s, sub).start()
-
-    half = SUBS // 2
-    long = (tuple(range(half)), tuple(range(half, SUBS)))
-    short = (long[1], long[0])
-
-    def ring_step(s, first):
-        for arm in (0, 1):
-            d = (8 - s) if arm == 0 else (8 + s)
-            c = lax.rem(o + d, NZ)
-            pair_got(c).wait_recv()
-            multiply(c, arm)
-        for i in range(half):
-            for arm in (0, 1):
-                pass_on(arm, s, long[arm][i], True)
-        for i in range(half):
-            for arm in (0, 1):
-                pass_on(arm, s, short[arm][i], not first)
-
-    def each(low, high, f):
-        def body(i, carry):
-            f(i)
-            return carry
-
-        lax.fori_loop(low, high, body, 0)
-
-    def ahead(s):
-        each(jnp.minimum(2 * s + AHEAD, NZ), jnp.minimum(2 * s + AHEAD + 2, NZ), plane_out)
-        each(2 * s + 1, jnp.minimum(2 * s + 3, NZ), fetch)
-
-    for p in range(PIECES):
-        for k in OTHERS:
-            line(k, p).start()
     tiles_copy.wait()
-    densify_range(0, EARLY)
     own_copy.wait()
-    each(0, AHEAD, plane_out)
-    densify_range(EARLY, 6)
+    densify_range(0, 5)
+    batch_out(0)
+    densify_range(5, 6)
+    batch_out(1)
     fetch(0)
     c0 = chunk(0)
     pair_got(c0).wait_recv()
@@ -228,8 +254,13 @@
             sub = long[arm][i]
             snd[arm, 0, sub] = own(0, sub).astype(BF16)
             hop(arm, 0, sub).start()
+    batch_sent(0)
+    batch_out(2)
     ahead(0)
     ring_step(1, True)
+    batch_sent(1)
+    batch_out(3)
+    batch_sent(2)
     ahead(1)
 
     def body(s, carry):
@@ -241,37 +272,41 @@
 
     pair_got(o).wait_recv()
     multiply(o, 0)
+    for p in range(PIECES):
+        for k in OTHERS:
+            line(k, p).wait_send()
+
+    def drain(c):
+        pair(c).wait_send()
+
+    each(0, NZ, drain)
+    batch_sent(3)
+    for arm in (0, 1):
+        for sub in long[arm]:
+            hop(arm, 0, sub).wait_send()
+
+    def drain_ring(s):
+        for arm in (0, 1):
+            for sub in range(SUBS):
+                hop(arm, s, sub).wait_send()
+
+    each(1, 7, drain_ring)
+
+    def written(sub):
+        part = pl.ds(sub * SUB, SUB)
+        return pltpu.make_async_copy(result.at[part], out_hbm.at[part], local_sem.at[3 + sub])
+
     for i in range(SUBS):
         sub = (long[0] + long[1])[i]
         hop(0, 7, sub).wait_recv()
         hop(1, 7, sub).wait_recv()
         value = own(0, sub) + rcv[0, 7, sub].astype(F32) + rcv[1, 7, sub].astype(F32)
-        out_ref[sub * SUB:(sub + 1) * SUB, :] = value.astype(BF16)
-
-    for p in range(PIECES):
-        for k in OTHERS:
-            line(k, p).wait_send()
-
-    def drain(c):
-        pair(c).wait_send()
-
-        @pl.when(steps_from(c)[1] == 0)
-        def _():
-            for p in range(PIECES):
-                for k in OTHERS:
-                    plane(c, k, p).wait_send()
-
-    each(0, NZ, drain)
-    for arm in (0, 1):
-        for sub in long[arm]:
-            hop(arm, 0, sub).wait_send()
-
-    def drain_ring(s):
-        for arm in (0, 1):
-            for sub in range(SUBS):
-                hop(arm, s, sub).wait_send()
-
-    each(1, 8, drain_ring)
+        result[sub * SUB:(sub + 1) * SUB, :] = value.astype(BF16)
+        written(sub).start()
+    for sub in range(SUBS):
+        written(sub).wait()
+
+    each(7, 8, drain_ring)
 
 
 def per_device(amplitudes, tiles, tile_map):
@@ -282,17 +317,19 @@
         in_specs=[
             pl.BlockSpec(memory_space=pltpu.HBM),
             pl.BlockSpec(memory_space=pltpu.HBM),
-            pl.BlockSpec(memory_space=pltpu.VMEM),
+            pl.BlockSpec(memory_space=pltpu.HBM),
         ],
-        out_specs=pl.BlockSpec(memory_space=pltpu.VMEM),
+        out_specs=pl.BlockSpec(memory_space=pltpu.HBM),
         scratch_shapes=[
             pltpu.VMEM((NZ, 2, SHARD, DEPTH), BF16),
             pltpu.VMEM((SLOTS, TILE * TILE), BF16),
+            pltpu.VMEM((1, SLOTS), jnp.int32),
+            pltpu.VMEM((2 * SHARD, WIDTH), BF16),
             pltpu.VMEM((DEPTH, WIDTH), BF16),
             pltpu.VMEM((2, 2 * SHARD, WIDTH), F32),
             pltpu.VMEM((2, 8, SUBS, SUB, WIDTH), BF16),
             pltpu.VMEM((2, 8, SUBS, SUB, WIDTH), BF16),
-            dma((2,)),
+            dma((3 + SUBS,)),
             dma((SIDE, PIECES)),
             dma((SIDE, PIECES)),
             dma((NZ, SIDE, PIECES)),

time: 79.6 us -> 76 us (0.955)
  Pallas kernels: 77.7 us -> 74.2 us
    pallas_call x1, Pallas kernels: 77.7 us -> 74.2 us  [per_device(): pl.pallas_call(kernel, out_shape=jax.ShapeDtypeStruct((2 * SHARD, WIDTH),...]
where the time goes in v3:
time: 76 us; the launch traced here: 75.8 us
  Pallas kernels  74.2 us (98%)
  local copies, waits for them, and re-layouts  1.62 us (2%)
    pallas_call x1, Pallas kernels, per_device(): pl.pallas_call(kernel, out_shape=jax.ShapeDtypeStruct((2 * SHARD, WIDTH),...  74.2 us
    unnamed x1, local copies, waits for them, and re-layouts  1.62 us

profile of v3, /device:TPU:1, one launch (start us, length us, event | category | flops | bytes accessed | tf_op | source)
XLA Modules:
  0.0 75.8 jit_solution(48600611656183621)
XLA Ops:
  0.0 74.2 %shard_map.37 = bf16[128,768]{1,0:T(8,128)(2,1)} custom-call(bf16[64,1536]{1,0:T(8,128)(2,1)} %a_hbm.1, bf16[48,9216]{1,0:T(8,128)(2,1)} %bitcast.2, s32[1,48]{1,0:T(1,128)} %bitcast.3), custom_call_target="tpu_custom_call" | custom-call | tf_op jit(solution)/shard_map/pallas_call | solution.py:314
  74.2 1.6 %copy.5 = bf16[128,768]{1,0:T(8,128)(2,1)} copy(bf16[128,768]{1,0:T(8,128)(2,1)} %shard_map.37) | data formatting | bytes 393216

commit v4 on v3

--- a/solution.py
+++ b/solution.py
@@ -16,6 +16,8 @@
 WIDTH = RES_TILES * TILE
 GROUP = 16
 PIECES = 2
+WINDOW = 3
+READY = 1
 PIECE = SHARD // PIECES
 SUBS = 4
 SUB = 2 * SHARD // SUBS
@@ -180,27 +182,32 @@
                 for k in OTHERS:
                     line(k, p).start()
 
-    def batch_out(place):
+    def item_out(q):
+        place, p = q // PIECES, q % PIECES
         for k in range(SIDE):
             @pl.when(places[k] == place)
             def _():
-                for p in range(PIECES):
-                    if k != 0:
-                        line_got(line_chips[k], SIDE - k, p).wait_recv()
-                    for j in OTHERS:
-                        plane(line_chips[k], j, p).start()
-
-    def batch_sent(place):
+                if k != 0:
+                    line_got(line_chips[k], SIDE - k, p).wait_recv()
+                for j in OTHERS:
+                    plane(line_chips[k], j, p).start()
+
+    def item_sent(q):
+        place, p = q // PIECES, q % PIECES
         for k in range(SIDE):
             @pl.when(places[k] == place)
             def _():
-                for p in range(PIECES):
-                    for j in OTHERS:
-                        plane(line_chips[k], j, p).wait_send()
-
-    def next_batch(i):
-        batch_sent(i - 1)
-        batch_out(i)
+                for j in OTHERS:
+                    plane(line_chips[k], j, p).wait_send()
+
+    ITEMS = SIDE * PIECES
+
+    def roll(low, high):
+        for q in range(low, high):
+            if q < ITEMS:
+                item_sent(q)
+            if q + WINDOW < ITEMS:
+                item_out(q + WINDOW)
 
     def ahead(s):
         each(2 * s + 1, jnp.minimum(2 * s + 3, NZ), fetch)
@@ -242,9 +249,10 @@
     tiles_copy.wait()
     own_copy.wait()
     densify_range(0, 5)
-    batch_out(0)
+    for q in range(WINDOW):
+        item_out(q)
     densify_range(5, 6)
-    batch_out(1)
+    roll(0, READY)
     fetch(0)
     c0 = chunk(0)
     pair_got(c0).wait_recv()
@@ -254,21 +262,22 @@
             sub = long[arm][i]
             snd[arm, 0, sub] = own(0, sub).astype(BF16)
             hop(arm, 0, sub).start()
-    batch_sent(0)
-    batch_out(2)
+    roll(READY, READY + PIECES)
     ahead(0)
     ring_step(1, True)
-    batch_sent(1)
-    batch_out(3)
-    batch_sent(2)
+    roll(READY + PIECES, READY + 2 * PIECES)
     ahead(1)
+
+    ring_step(2, False)
+    roll(READY + 2 * PIECES, ITEMS)
+    ahead(2)
 
     def body(s, carry):
         ring_step(s, False)
         ahead(s)
         return carry
 
-    lax.fori_loop(2, 8, body, 0)
+    lax.fori_loop(3, 8, body, 0)
 
     pair_got(o).wait_recv()
     multiply(o, 0)
@@ -280,7 +289,6 @@
         pair(c).wait_send()
 
     each(0, NZ, drain)
-    batch_sent(3)
     for arm in (0, 1):
         for sub in long[arm]:
             hop(arm, 0, sub).wait_send()

time: 76 us -> 76 us (level)
  no operation moved by 1% of the time
where the time goes in v4:
time: 76 us; the launch traced here: 75.9 us
  Pallas kernels  74.3 us (98%)
  local copies, waits for them, and re-layouts  1.62 us (2%)
    pallas_call x1, Pallas kernels, per_device(): pl.pallas_call(kernel, out_shape=jax.ShapeDtypeStruct((2 * SHARD, WIDTH),...  74.3 us
    unnamed x1, local copies, waits for them, and re-layouts  1.62 us

profile of v4, /device:TPU:1, one launch (start us, length us, event | category | flops | bytes accessed | tf_op | source)
XLA Modules:
  0.0 75.9 jit_solution(9954233676110803711)
XLA Ops:
  0.0 74.3 %shard_map.37 = bf16[128,768]{1,0:T(8,128)(2,1)} custom-call(bf16[64,1536]{1,0:T(8,128)(2,1)} %a_hbm.1, bf16[48,9216]{1,0:T(8,128)(2,1)} %bitcast.2, s32[1,48]{1,0:T(1,128)} %bitcast.3), custom_call_target="tpu_custom_call" | custom-call | tf_op jit(solution)/shard_map/pallas_call | solution.py:322
  74.3 1.6 %copy.5 = bf16[128,768]{1,0:T(8,128)(2,1)} copy(bf16[128,768]{1,0:T(8,128)(2,1)} %shard_map.37) | data formatting | bytes 393216

commit v5 on v4

--- a/solution.py
+++ b/solution.py
@@ -64,13 +64,13 @@
     tiles_copy = pltpu.make_async_copy(tiles_hbm, tiles_v, local_sem.at[0])
     own_copy = pltpu.make_async_copy(a_hbm, a_all.at[chip, h], local_sem.at[1])
     map_copy = pltpu.make_async_copy(map_hbm, map_ref, local_sem.at[2])
+
+    barrier = pltpu.get_barrier_semaphore()
+    for device in [on_line(k) for k in OTHERS] + [on_plane(k) for k in OTHERS] + [mate, *ring]:
+        pl.semaphore_signal(barrier, inc=1, device_id=device, device_id_type=MESH)
     map_copy.start()
     tiles_copy.start()
     own_copy.start()
-
-    barrier = pltpu.get_barrier_semaphore()
-    for device in [on_line(k) for k in OTHERS] + [on_plane(k) for k in OTHERS] + [mate, *ring]:
-        pl.semaphore_signal(barrier, inc=1, device_id=device, device_id_type=MESH)
     pl.semaphore_wait(barrier, 9)
 
     def rows(p):

time: 76 us -> 76 us (level)
  no operation moved by 1% of the time
where the time goes in v5:
time: 76 us; the launch traced here: 75.9 us
  Pallas kernels  74.2 us (98%)
  local copies, waits for them, and re-layouts  1.62 us (2%)
    pallas_call x1, Pallas kernels, per_device(): pl.pallas_call(kernel, out_shape=jax.ShapeDtypeStruct((2 * SHARD, WIDTH),...  74.2 us
    unnamed x1, local copies, waits for them, and re-layouts  1.62 us

profile of v5, /device:TPU:1, one launch (start us, length us, event | category | flops | bytes accessed | tf_op | source)
XLA Modules:
  0.0 75.9 jit_solution(6815719832418635678)
XLA Ops:
  0.0 74.2 %shard_map.37 = bf16[128,768]{1,0:T(8,128)(2,1)} custom-call(bf16[64,1536]{1,0:T(8,128)(2,1)} %a_hbm.1, bf16[48,9216]{1,0:T(8,128)(2,1)} %bitcast.2, s32[1,48]{1,0:T(1,128)} %bitcast.3), custom_call_target="tpu_custom_call" | custom-call | tf_op jit(solution)/shard_map/pallas_call | solution.py:322
  74.3 1.6 %copy.5 = bf16[128,768]{1,0:T(8,128)(2,1)} copy(bf16[128,768]{1,0:T(8,128)(2,1)} %shard_map.37) | data formatting | bytes 393216
